TPU v7x, 32 devices: a whole 2x2x4 slice. The times are simulated.
32 devices in a mesh: ad: 8 (over z, core), tp: 4 (over y, x).
Axes of the slice: x: 2, y: 2, z: 4, core: 2. Of those that a mesh axis runs over, the one named last changes fastest.
Arguments:
- tokens: bfloat16 [1024, 8192], P('ad', 'tp'), may hold values from -6 to 6
- query_weight: bfloat16 [8192, 8192], P(None, 'tp'), may hold values from -0.0625 to 0.0625
- adapter_down_weight: bfloat16 [128, 8192, 64], P('ad', 'tp'), may hold values from -0.0625 to 0.0625
- adapter_up_weight: bfloat16 [128, 64, 8192], P('ad', None, 'tp'), may hold values from -0.75 to 0.75
- row_adapter_index: int32 [1024], P('ad'), may hold values from 0 to 127, as said below
- adapter_table_slot: int32 [128], replicated, may hold values from 0 to 127, as said below
- lengths: int32 [1024], P('ad'), may hold values from 1 to 64, as said below
- cached_key_rows: bfloat16 [1024, 8, 64, 128], P('ad', None, 'tp'), may hold values from -360 to 360
- cached_value_rows: bfloat16 [1024, 8, 64, 128], P('ad', None, 'tp'), may hold values from -6 to 6
Outputs:
- queries: bfloat16 [1024, 8192], P('ad', 'tp')
- attended: bfloat16 [1024, 8192], P('ad', 'tp')
Inputs may be any that keep to these rules, and one draw needn't show every extreme that they name: `row_adapter_index`: within each aligned block of 128 rows at most 48 rows have their adapter's slot in any one run of 16 slots (slot // 16); one such run, drawn from the seed, is named by exactly 48 rows of every block. `adapter_table_slot`: A permutation of the slots. `lengths`: some row has exactly 64 and some row exactly 1.
All inputs are finite; a program needn't handle non-finite values.
Results may differ from a plain program's by a relative error of at most 0.019.
Values may be sent and summed in bfloat16 or wider, within the bound.
A program may use at most 128 MiB of HBM per device.

v0:
```python
import math
import jax
import jax.numpy as jnp
from jax import lax
from jax.sharding import PartitionSpec as P


def rotate(query, lengths):
    head_dim = query.shape[-1]
    half = head_dim // 2
    freq = jnp.exp(jnp.arange(half, dtype=jnp.float32) * (-2.0 * math.log(500000.0) / head_dim))
    angle = (lengths - 1).astype(jnp.float32)[:, None, None] * freq[None, None, :]
    cosine = jnp.cos(angle)
    sine = jnp.sin(angle)
    first = query[..., :half]
    second = query[..., half:]
    return jnp.concatenate(
        [first * cosine - second * sine, second * cosine + first * sine], axis=-1
    )


def lookup(ids, adapter_table_slot):
    table = jnp.arange(adapter_table_slot.shape[0], dtype=jnp.int32)
    return jnp.sum(
        jnp.where(ids[:, None] == table[None, :], adapter_table_slot[None, :], 0), axis=1
    )


def shrink_rows(input_rows, local_partial, adapter_down_weight):
    adapter_row_count = adapter_down_weight.shape[0]
    select_rows = (
        local_partial[:, None] == jnp.arange(adapter_row_count, dtype=jnp.int32)[None, :]
    ).astype(jnp.float32)
    update_terms = jnp.einsum(
        "nt,vtm->nvm", input_rows, adapter_down_weight, preferred_element_type=jnp.float32
    )
    return (select_rows, jnp.sum(update_terms * select_rows[:, :, None], axis=1))


def expand_rows(select_rows, reduced_rows, adapter_up_weight):
    spread_rows = (select_rows[:, :, None] * reduced_rows.astype(jnp.float32)[:, None, :]).astype(
        jnp.bfloat16
    )
    return jnp.einsum(
        "pow,owu->pu", spread_rows, adapter_up_weight, preferred_element_type=jnp.float32
    ).astype(jnp.bfloat16)


def per_device(
    tokens,
    query_weight,
    adapter_down_weight,
    adapter_up_weight,
    row_adapter_index,
    adapter_table_slot,
    lengths,
    cached_key_rows,
    cached_value_rows,
):
    rows = tokens.shape[0]
    columns = query_weight.shape[1]
    tp_count = lax.axis_size("tp")
    owner_partials = adapter_down_weight.shape[0]
    base = jnp.dot(
        lax.all_gather(tokens, "tp", axis=1, tiled=True),
        query_weight,
        preferred_element_type=jnp.float32,
    )
    combined_output, every_id = (
        lax.all_gather(tokens, "ad", axis=0, tiled=True),
        lax.all_gather(row_adapter_index, "ad", axis=0, tiled=True),
    )
    slots = lookup(every_id, adapter_table_slot)
    mine = slots // owner_partials == lax.axis_index("ad")
    local_partial = jnp.where(mine, slots % owner_partials, -1)
    select_rows, partial_value_sum = shrink_rows(
        combined_output, local_partial, adapter_down_weight
    )
    reduced_rows = lax.psum(partial_value_sum, "tp").astype(jnp.bfloat16)
    lowrank_change = expand_rows(select_rows, reduced_rows, adapter_up_weight)
    delta = lax.psum_scatter(
        lowrank_change.astype(jnp.float32).astype(jnp.bfloat16),
        "ad",
        scatter_dimension=0,
        tiled=True,
    ).astype(jnp.float32)
    head_dim = cached_key_rows.shape[3]
    query = (base + delta).reshape(rows, columns // head_dim, head_dim)
    queries = rotate(query, lengths).reshape(rows, columns).astype(jnp.bfloat16)
    every_head = lax.all_gather(queries, "tp", axis=1, tiled=True)
    kv_heads = cached_key_rows.shape[1]
    span = cached_key_rows.shape[2]
    grouped = every_head.reshape(rows, kv_heads, -1, head_dim)
    scores = jnp.einsum(
        "rkgd,rkpd->rkgp", grouped, cached_key_rows, preferred_element_type=jnp.float32
    ) * (1.0 / math.sqrt(head_dim))
    position = lax.axis_index("tp") * span + jnp.arange(span, dtype=jnp.int32)
    valid = (position[None, :] < lengths[:, None])[:, None, None, :]
    scores = jnp.where(valid, scores, -1e30)
    peak = jnp.max(scores, axis=-1)
    weights = jnp.where(valid, jnp.exp(scores - peak[..., None]), 0.0)
    total = jnp.sum(weights, axis=-1)
    partial_out = jnp.einsum(
        "rkgp,rkpd->rkgd",
        weights.astype(jnp.bfloat16),
        cached_value_rows,
        preferred_element_type=jnp.float32,
    ).astype(jnp.bfloat16)
    peaks, totals = (
        lax.all_to_all(
            peak.reshape(rows, tp_count, -1), "tp", split_axis=1, concat_axis=1, tiled=True
        ),
        lax.all_to_all(
            total.reshape(rows, tp_count, -1), "tp", split_axis=1, concat_axis=1, tiled=True
        ),
    )
    partials = lax.all_to_all(
        partial_out.reshape(rows, tp_count, -1), "tp", split_axis=1, concat_axis=1, tiled=True
    )
    highest = jnp.max(peaks, axis=1, keepdims=True)
    factor = jnp.exp(peaks - highest)
    numer = jnp.sum(
        factor[..., None] * partials.reshape(rows, tp_count, -1, head_dim).astype(jnp.float32),
        axis=1,
    )
    denom = jnp.sum(factor * totals, axis=1)
    attended = (numer / denom[..., None]).reshape(rows, columns).astype(jnp.bfloat16)
    return (queries, attended)


def solution(mesh):
    return jax.shard_map(
        per_device,
        mesh=mesh,
        in_specs=(
            P("ad", "tp"),
            P(None, "tp"),
            P("ad", "tp", None),
            P("ad", None, "tp"),
            P("ad"),
            P(),
            P("ad"),
            P("ad", None, "tp", None),
            P("ad", None, "tp", None),
        ),
        out_specs=(P("ad", "tp"), P("ad", "tp")),
        check_vma=False,
    )
```

profile of v0, /device:TPU:0, one launch (start us, length us, event | category | flops | bytes accessed | tf_op | source)
XLA Modules:
  0.0 274.9 jit_solution(6826846657034868188)
XLA Ops:
  8.7 13.5 %all-gather = s32[8,1,128]{2,1,0:T(1,128)S(1)} all-gather(s32[1,1,128]{2,1,0:T(1,128)} %bitcast.48), channel_id=1, replica_groups=mesh['ad'=8,'tp'=4] {'ad'}, dimensions={0}, use_global_device_ids=true | all-gather | bytes 4608 | tf_op jit(solution)/shard_map/all_gather | solution.py:71
  22.2 1.0 select_reduce_fusion
  23.3 36.2 %all-gather.7.cloned.1.call-done = bf16[1024,2048]{1,0:T(8,128)(2,1)} async-done(((bf16[128,2048]{1,0:T(8,128)(2,1)}), bf16[1024,2048]{1,0:T(8,128)(2,1)}) %all-gather.7.cloned.1.call-update) | async-done | bytes 4194320 | tf_op jit(solution)/shard_map/all_gather | solution.py:70
  59.5 7.6 %fusion.25 = f32[1024,1024]{0,1:S(1)} fusion(bf16[1024,2048]{1,0:T(8,128)(2,1)} %all-gather.7.cloned.1.call-done, bf16[2048,1024]{0,1:T(8,128)(2,1)} %bitcast.49), kind=kOutput, calls=%fused_computation.52 | convolution fusion | flops 4294967296 | bytes 12582912
  67.6 25.3 %all-reduce.1 = bf16[1024,64]{0,1:T(8,128)(2,1)S(1)} all-reduce(f32[1024,64]{0,1:T(8,128)S(1)} %multiply_reduce_fusion.1), channel_id=1, replica_groups=mesh['ad'=8,'tp'=4] {'tp'}, use_global_device_ids=true, to_apply=%region_2.3 | all-reduce | flops 65536 | bytes 393216 | tf_op jit(solution)/shard_map/psum | solution.py:79
  93.0 8.3 %bitcast_convert_fusion = bf16[1024,2048]{1,0:T(8,128)(2,1)} fusion(bf16[16,64,2048]{2,1,0:T(8,128)(2,1)} %param.12, f32[1024,64]{0,1:T(8,128)S(1)} %convert_element_type.71, f32[1024,16]{0,1:T(8,128)S(1)} %fusion.17), kind=kOutput, calls=%fused_computation | convolution fusion | flops 4299161600 | bytes 8716288 | tf_op jit(solution)/shard_map/pow,owu->pu/dot_general | solution.py:44
  102.3 49.9 %reduce-scatter.2.cloned.1.call-done = bf16[128,2048]{1,0:T(8,128)(2,1)} async-done(((bf16[1024,2048]{1,0:T(8,128)(2,1)}), bf16[128,2048]{1,0:T(8,128)(2,1)}) %reduce-scatter.2.cloned.1.call-update) | async-done | bytes 524304 | tf_op jit(solution)/shard_map/reduce_scatter | solution.py:81
  152.1 15.7 %fusion.15 = f32[16,8,16,128]{3,1,2,0:T(8,128)S(1)} fusion(bf16[128,8192]{1,0:T(8,128)(2,1)} %all-gather.5.cloned.1.call-done, bf16[8192,2048]{1,0:T(8,128)(2,1)} %param.10, bf16[128,2048]{1,0:T(8,128)(2,1)} %reduce-scatter.2.cloned.1.call-done), kind=kOutput, calls=%fused_computation.19 | convolution fusion | flops 4295491584 | bytes 37224448 | tf_op jit(solution)/shard_map/dot_general | solution.py:64
  168.9 0.9 copy.29
  169.9 33.5 %all-gather.9.cloned.1.call-done = bf16[128,8192]{1,0:T(8,128)(2,1)} async-done(((bf16[128,2048]{1,0:T(8,128)(2,1)}), bf16[128,8192]{1,0:T(8,128)(2,1)}) %all-gather.9.cloned.1.call-update) | async-done | bytes 2097168 | tf_op jit(solution)/shard_map/all_gather | solution.py:90
  203.4 2.3 copy.25
  206.3 4.2 %fusion = (f32[128,8,8]{2,1,0:T(8,128)S(1)}, f32[128,8,8,16]{3,2,1,0:T(8,128)}) fusion(pred[128,16]{1,0:T(8,128)(4,1)S(1)} %broadcast_compare_fusion, bf16[128,8,8,128]{3,2,1,0:T(8,128)(2,1)S(1)} %bitcast.40, bf16[128,8,16,128]{3,2,1,0:T(8,128)(2,1)S(1)} %copy-done), kind=kOutput, calls=%fused_computation.6 | convolution fusion | flops 33939456 | bytes 6850560 | tf_op jit(solution)/shard_map/rkgd,rkpd->rkgp/dot_general | solution.py:94
  211.3 3.3 %all-to-all-start = ((f32[128,4,16]{0,2,1:T(8,128)}), f32[128,4,16]{0,2,1:T(8,128)S(1)}, u32[]{:S(2)}, u32[]{:S(2)}) async-start(f32[128,4,16]{0,2,1:T(8,128)} %bitcast.6), calls=%async_computation.1 | async-start | bytes 65536 | tf_op jit(solution)/shard_map/all_to_all | solution.py:110
  214.6 4.7 %fusion.1 = f32[128,8,8]{2,1,0:T(8,128)S(1)} fusion(f32[128,8,8,16]{3,2,1,0:T(8,128)} %get-tuple-element.9, f32[128,8,8]{2,1,0:T(8,128)S(1)} %get-tuple-element.8, pred[128,16]{1,0:T(8,128)(4,1)S(1)} %broadcast_compare_fusion), kind=kLoop, calls=%fused_computation.7 | loop fusion | flops 647168 | bytes 591872 | tf_op jit(solution)/shard_map/reduce_sum | solution.py:102
  220.1 4.2 %all-to-all-start.2 = ((f32[128,4,16]{0,2,1:T(8,128)}), f32[128,4,16]{0,2,1:T(8,128)S(1)}, u32[]{:S(2)}, u32[]{:S(2)}) async-start(f32[128,4,16]{0,2,1:T(8,128)} %bitcast.7), calls=%async_computation.3 | async-start | bytes 65536 | tf_op jit(solution)/shard_map/all_to_all | solution.py:113
  224.3 6.4 %fusion.12 = bf16[128,8,8,128]{3,2,1,0:T(8,128)(2,1)} fusion(bf16[128,8,16,128]{3,2,1,0:T(8,128)(2,1)} %param.17, f32[128,8,8,16]{3,2,1,0:T(8,128)} %get-tuple-element.9, f32[128,8,8]{2,1,0:T(8,128)S(1)} %get-tuple-element.8, pred[128,16]{1,0:T(8,128)(4,1)S(1)} %broadcast_compare_fusion), kind=kOutput, calls=%fused_computation.18 | convolution fusion | flops 35258368 | bytes 6850560 | tf_op jit(solution)/shard_map/rkgp,rkpd->rkgd/dot_general | solution.py:103
  230.6 2.5 reshape.175
  233.2 2.5 copy.20
  235.7 4.2 %all-to-all-start.1 = ((bf16[128,4,2048]{2,0,1:T(8,128)(2,1)}), bf16[128,4,2048]{2,0,1:T(8,128)(2,1)S(1)}, u32[]{:S(2)}, u32[]{:S(2)}) async-start(bf16[128,4,2048]{2,0,1:T(8,128)(2,1)} %copy.20), calls=%async_computation.2 | async-start | bytes 4194304 | tf_op jit(solution)/shard_map/all_to_all | solution.py:117
  240.2 2.6 mul.119
  242.8 4.9 %mul.120 = f32[128,4,2048]{2,0,1:T(8,128)} reshape(f32[128,4,16,128]{3,2,0,1:T(8,128)} %mul.119) | data formatting | bytes 8388608 | tf_op jit(solution)/shard_map/mul | solution.py:123
  247.7 16.3 %all-to-all-done.1 = bf16[128,4,2048]{2,0,1:T(8,128)(2,1)S(1)} async-done(((bf16[128,4,2048]{2,0,1:T(8,128)(2,1)}), bf16[128,4,2048]{2,0,1:T(8,128)(2,1)S(1)}, u32[]{:S(2)}, u32[]{:S(2)}) %all-to-all-start.1) | async-done | bytes 2097184 | tf_op jit(solution)/shard_map/all_to_all | solution.py:117
  264.0 2.9 %multiply_reduce_fusion = f32[128,2048]{1,0:T(8,128)S(1)} fusion(f32[128,4,2048]{2,0,1:T(8,128)} %mul.120, bf16[128,4,2048]{2,0,1:T(8,128)(2,1)S(1)} %all-to-all-done.1), kind=kLoop, calls=%fused_computation.1 | loop fusion | flops 2883584 | bytes 7340032 | tf_op jit(solution)/shard_map/reduce_sum | solution.py:122
  267.2 1.2 fusion.16
  (34 shorter events, 6.9 us)
Async XLA Ops:
  7.2 52.3 %all-gather.7.cloned.1.call-start = ((), (), s32[]{:S(2)}) async-start(), calls=%async_computation.5 | async-start | bytes 4718592 | tf_op jit(solution)/shard_map/all_gather | solution.py:70
  7.9 94.4 %all-gather.5.cloned.1.call-start = ((), (), s32[]{:S(2)}) async-start(), calls=%async_computation.4 | async-start | bytes 2621440 | tf_op jit(solution)/shard_map/all_gather | solution.py:65
  8.6 143.5 %reduce-scatter.2.cloned.1.call-start = ((), (), s32[]{:S(2)}) async-start(), calls=%async_computation.6 | async-start | bytes 4718592 | tf_op jit(solution)/shard_map/reduce_scatter | solution.py:81
  101.3 0.7 copy-start.1
  101.3 102.1 %all-gather.9.cloned.1.call-start = ((), (), s32[]{:S(2)}) async-start(), calls=%async_computation.7 | async-start | bytes 2621440 | tf_op jit(solution)/shard_map/all_gather | solution.py:90
  203.4 2.8 %copy-start = (bf16[128,8,16,128]{3,2,1,0:T(8,128)(2,1)S(1)}, bf16[128,8,16,128]{3,2,1,0:T(8,128)(2,1)}, u32[]{:S(2)}) copy-start(bf16[128,8,16,128]{3,2,1,0:T(8,128)(2,1)} %param.16) | copy-start | bytes 12582916
  211.3 8.8 %all-to-all-start = ((f32[128,4,16]{0,2,1:T(8,128)}), f32[128,4,16]{0,2,1:T(8,128)S(1)}, u32[]{:S(2)}, u32[]{:S(2)}) async-start(f32[128,4,16]{0,2,1:T(8,128)} %bitcast.6), calls=%async_computation.1 | async-start | bytes 65536 | tf_op jit(solution)/shard_map/all_to_all | solution.py:110
  220.1 15.6 %all-to-all-start.2 = ((f32[128,4,16]{0,2,1:T(8,128)}), f32[128,4,16]{0,2,1:T(8,128)S(1)}, u32[]{:S(2)}, u32[]{:S(2)}) async-start(f32[128,4,16]{0,2,1:T(8,128)} %bitcast.7), calls=%async_computation.3 | async-start | bytes 65536 | tf_op jit(solution)/shard_map/all_to_all | solution.py:113
  235.7 28.2 %all-to-all-start.1 = ((bf16[128,4,2048]{2,0,1:T(8,128)(2,1)}), bf16[128,4,2048]{2,0,1:T(8,128)(2,1)S(1)}, u32[]{:S(2)}, u32[]{:S(2)}) async-start(bf16[128,4,2048]{2,0,1:T(8,128)(2,1)} %copy.20), calls=%async_computation.2 | async-start | bytes 4194304 | tf_op jit(solution)/shard_map/all_to_all | solution.py:117
Sparse Core Ops, SparseCore 0:
  9.6 49.8 all-gather.6
  61.3 38.7 all-gather.4
  102.4 49.6 reduce-scatter.1
  169.9 33.4 all-gather.8
where the time goes:
time: 276 us; the launch traced here: 275 us
  waiting for transfers between devices  137 us (50%)
  matrix products  42.2 us (15%)
  blocking collectives  38.9 us (14%)
  local copies, waits for them, and re-layouts  19 us (7%)
  between operations  13.9 us (5%)
  starting transfers between devices  11.9 us (4%)
  other arithmetic  11.7 us (4%)
    reduce_scatter x1, waiting for transfers between devices, per_device(): lax.psum_scatter(lowrank_change.astype(jnp.float32).astype(jnp.bfloat16),...  49.9 us
    all_gather x1, waiting for transfers between devices, per_device(): lax.all_gather(tokens, 'ad', axis=0, tiled=True)  36.2 us
    all_gather x1, waiting for transfers between devices, per_device(): every_head = lax.all_gather(queries, 'tp', axis=1, tiled=True)  33.5 us
    psum x1, blocking collectives, per_device(): reduced_rows = lax.psum(partial_value_sum, 'tp').astype(jnp.bfloat16)  25.3 us
    all_to_all x1, waiting for transfers between devices, per_device(): lax.all_to_all(partial_out.reshape(rows, tp_count, -1), 'tp', split_axis=...  16.3 us
    dot_general x1, matrix products, per_device(): jnp.dot(lax.all_gather(tokens, 'tp', axis=1, tiled=True), query_weight, p...  15.7 us
    all_gather x1, blocking collectives, per_device(): lax.all_gather(row_adapter_index, 'ad', axis=0, tiled=True)  13.5 us
    dot_general x1, matrix products, expand_rows(): jnp.einsum('pow,owu->pu', spread_rows, adapter_up_weight, preferred_eleme...  8.29 us
  transfers between devices with their start and end apart: 7, of which 4 were waited for; matrix products, arithmetic and copies ran while one was open for 15% of the time, Pallas kernels for 0%

commit v1 on v0

--- a/solution.py
+++ b/solution.py
@@ -87,7 +87,21 @@
     head_dim = cached_key_rows.shape[3]
     query = (base + delta).reshape(rows, columns // head_dim, head_dim)
     queries = rotate(query, lengths).reshape(rows, columns).astype(jnp.bfloat16)
-    every_head = lax.all_gather(queries, "tp", axis=1, tiled=True)
+    ways, here, turn = (lax.axis_size("tp"), lax.axis_index("tp"), queries.shape[1])
+    lengths_2 = [n * ways if d == 1 else n for d, n in enumerate(queries.shape)]
+    full = lax.dynamic_update_slice_in_dim(
+        jnp.zeros(lengths_2, queries.dtype), queries, here * turn, axis=1
+    )
+    going_up = going_down = queries
+    for far in range(1, ways // 2 + 1):
+        going_up = lax.ppermute(going_up, "tp", [(d, (d + 1) % ways) for d in range(ways)])
+        full = lax.dynamic_update_slice_in_dim(full, going_up, (here - far) % ways * turn, axis=1)
+        if 2 * far < ways:
+            going_down = lax.ppermute(going_down, "tp", [(d, (d - 1) % ways) for d in range(ways)])
+            full = lax.dynamic_update_slice_in_dim(
+                full, going_down, (here + far) % ways * turn, axis=1
+            )
+    every_head = full
     kv_heads = cached_key_rows.shape[1]
     span = cached_key_rows.shape[2]
     grouped = every_head.reshape(rows, kv_heads, -1, head_dim)

time: 276 us -> 275 us (level)
  waiting for transfers between devices: 137 us -> 134 us
    all_gather x1 -> x0, waiting for transfers between devices: 33.5 us -> none  [per_device(): every_head = lax.all_gather(queries, 'tp', axis=1, tiled=True)]
    ppermute x0 -> x3, waiting for transfers between devices: none -> 30.2 us  [the longest x2 19.6 us: per_device(): lax.ppermute(going_up, 'tp', [(d, (d + 1) % ways) for d in range(ways)])]
    all_to_all x1, waiting for transfers between devices: 0.01 us -> 3.91 us  [per_device(): lax.all_to_all(total.reshape(rows, tp_count, -1), 'tp', split_axis=1, con...]
    all_to_all x1, waiting for transfers between devices: 16.3 us -> 12.6 us  [per_device(): lax.all_to_all(partial_out.reshape(rows, tp_count, -1), 'tp', split_axis=...]
    ppermute x0 -> x3, starting transfers between devices: none -> 3.53 us  [the longest x2 2.05 us: per_device(): lax.ppermute(going_up, 'tp', [(d, (d + 1) % ways) for d in range(ways)])]
  transfers between devices with their start and end apart: 7 -> 9, of which waited for: 4 -> 7; matrix products, arithmetic and copies ran while one was open for 15% -> 14% of each run, Pallas kernels for 0% -> 0%
where the time goes in v1:
time: 275 us; the launch traced here: 272 us
  waiting for transfers between devices  134 us (49%)
  matrix products  40.3 us (15%)
  blocking collectives  39 us (14%)
  local copies, waits for them, and re-layouts  20.6 us (7%)
  starting transfers between devices  14.3 us (5%)
  between operations  14.1 us (5%)
  other arithmetic  10 us (4%)
    reduce_scatter x1, waiting for transfers between devices, per_device(): lax.psum_scatter(lowrank_change.astype(jnp.float32).astype(jnp.bfloat16),...  49.6 us
    all_gather x1, waiting for transfers between devices, per_device(): lax.all_gather(tokens, 'ad', axis=0, tiled=True)  36.2 us
    psum x1, blocking collectives, per_device(): reduced_rows = lax.psum(partial_value_sum, 'tp').astype(jnp.bfloat16)  25.5 us
    ppermute x2, waiting for transfers between devices, per_device(): lax.ppermute(going_up, 'tp', [(d, (d + 1) % ways) for d in range(ways)])  19.6 us
    dot_general x1, matrix products, per_device(): jnp.dot(lax.all_gather(tokens, 'tp', axis=1, tiled=True), query_weight, p...  15.7 us
    all_gather x1, blocking collectives, per_device(): lax.all_gather(row_adapter_index, 'ad', axis=0, tiled=True)  13.5 us
    all_to_all x1, waiting for transfers between devices, per_device(): lax.all_to_all(partial_out.reshape(rows, tp_count, -1), 'tp', split_axis=...  12.6 us
    ppermute x1, waiting for transfers between devices, per_device(): lax.ppermute(going_down, 'tp', [(d, (d - 1) % ways) for d in range(ways)])  10.6 us
  transfers between devices with their start and end apart: 9, of which 7 were waited for; matrix products, arithmetic and copies ran while one was open for 14% of the time, Pallas kernels for 0%

profile of v1, /device:TPU:0, one launch (start us, length us, event | category | flops | bytes accessed | tf_op | source)
XLA Modules:
  0.0 272.2 jit_solution(11745062555348634196)
XLA Ops:
  8.7 13.5 %all-gather = s32[8,1,128]{2,1,0:T(1,128)S(1)} all-gather(s32[1,1,128]{2,1,0:T(1,128)} %bitcast.46), channel_id=1, replica_groups=mesh['ad'=8,'tp'=4] {'ad'}, dimensions={0}, use_global_device_ids=true | all-gather | bytes 4608 | tf_op jit(solution)/shard_map/all_gather | solution.py:71
  23.3 36.2 %all-gather.6.cloned.1.call-done = bf16[1024,2048]{1,0:T(8,128)(2,1)} async-done(((bf16[128,2048]{1,0:T(8,128)(2,1)}), bf16[1024,2048]{1,0:T(8,128)(2,1)}) %all-gather.6.cloned.1.call-update) | async-done | bytes 4194320 | tf_op jit(solution)/shard_map/all_gather | solution.py:70
  59.5 7.6 %fusion.25 = f32[1024,1024]{0,1:S(1)} fusion(bf16[1024,2048]{1,0:T(8,128)(2,1)} %all-gather.6.cloned.1.call-done, bf16[2048,1024]{0,1:T(8,128)(2,1)} %bitcast.47), kind=kOutput, calls=%fused_computation.56 | convolution fusion | flops 4294967296 | bytes 12582912
  67.6 25.5 %all-reduce.1 = bf16[1024,64]{0,1:T(8,128)(2,1)S(1)} all-reduce(f32[1024,64]{0,1:T(8,128)S(1)} %multiply_reduce_fusion.1), channel_id=1, replica_groups=mesh['ad'=8,'tp'=4] {'tp'}, use_global_device_ids=true, to_apply=%region_2.3 | all-reduce | flops 65536 | bytes 393216 | tf_op jit(solution)/shard_map/psum | solution.py:79
  93.1 8.3 %bitcast_convert_fusion = bf16[1024,2048]{1,0:T(8,128)(2,1)} fusion(bf16[16,64,2048]{2,1,0:T(8,128)(2,1)} %param.12, f32[1024,64]{0,1:T(8,128)S(1)} %convert_element_type.71, f32[1024,16]{0,1:T(8,128)S(1)} %fusion.17), kind=kOutput, calls=%fused_computation | convolution fusion | flops 4299161600 | bytes 8716288 | tf_op jit(solution)/shard_map/pow,owu->pu/dot_general | solution.py:44
  102.4 49.6 %reduce-scatter.2.cloned.1.call-done = bf16[128,2048]{1,0:T(8,128)(2,1)} async-done(((bf16[1024,2048]{1,0:T(8,128)(2,1)}), bf16[128,2048]{1,0:T(8,128)(2,1)}) %reduce-scatter.2.cloned.1.call-update) | async-done | bytes 524304 | tf_op jit(solution)/shard_map/reduce_scatter | solution.py:81
  152.0 15.7 %fusion.15 = f32[16,8,16,128]{3,1,2,0:T(8,128)S(1)} fusion(bf16[128,8192]{1,0:T(8,128)(2,1)} %all-gather.4.cloned.1.call-done, bf16[8192,2048]{1,0:T(8,128)(2,1)} %param.10, bf16[128,2048]{1,0:T(8,128)(2,1)} %reduce-scatter.2.cloned.1.call-done), kind=kOutput, calls=%fused_computation.19 | convolution fusion | flops 4295491584 | bytes 37224448 | tf_op jit(solution)/shard_map/dot_general | solution.py:64
  172.1 12.8 %collective-permute-done = bf16[128,2048]{1,0:T(8,128)(2,1)S(1)} collective-permute-done((bf16[128,2048]{1,0:T(8,128)(2,1)S(1)}, bf16[128,2048]{1,0:T(8,128)(2,1)S(1)}, u32[]{:S(2)}, u32[]{:S(2)}) %collective-permute-start) | collective-permute-done | bytes 524320 | tf_op jit(solution)/shard_map/ppermute | solution.py:97
  185.7 10.6 %collective-permute-done.1 = bf16[128,2048]{1,0:T(8,128)(2,1)} collective-permute-done((bf16[128,2048]{1,0:T(8,128)(2,1)S(1)}, bf16[128,2048]{1,0:T(8,128)(2,1)}, u32[]{:S(2)}, u32[]{:S(2)}) %collective-permute-start.1) | collective-permute-done | bytes 524320 | tf_op jit(solution)/shard_map/ppermute | solution.py:100
  197.3 6.8 %collective-permute-done.2 = bf16[128,2048]{1,0:T(8,128)(2,1)} collective-permute-done((bf16[128,2048]{1,0:T(8,128)(2,1)S(1)}, bf16[128,2048]{1,0:T(8,128)(2,1)}, u32[]{:S(2)}, u32[]{:S(2)}) %collective-permute-start.2) | collective-permute-done | bytes 524320 | tf_op jit(solution)/shard_map/ppermute | solution.py:97
  205.8 2.4 fusion
  208.2 1.9 copy-done
  210.1 3.1 %fusion.1 = f32[128,8,8]{2,1,0:T(8,128)S(1)} fusion(f32[128,8,8,16]{3,2,1,0:T(8,128)S(1)} %get-tuple-element.11, f32[128,8,8]{2,1,0:T(8,128)S(1)} %get-tuple-element.10, pred[128,16]{1,0:T(8,128)(4,1)S(1)} %broadcast_compare_fusion), kind=kLoop, calls=%fused_computation.7 | loop fusion | flops 647168 | bytes 591872 | tf_op jit(solution)/shard_map/reduce_sum | solution.py:116
  214.0 3.3 %all-to-all-start.2 = ((f32[128,4,16]{0,2,1:T(8,128)}), f32[128,4,16]{0,2,1:T(8,128)S(1)}, u32[]{:S(2)}, u32[]{:S(2)}) async-start(f32[128,4,16]{0,2,1:T(8,128)} %bitcast.7), calls=%async_computation.3 | async-start | bytes 65536 | tf_op jit(solution)/shard_map/all_to_all | solution.py:127
  218.1 3.9 %all-to-all-done.2 = f32[128,4,16]{0,2,1:T(8,128)S(1)} async-done(((f32[128,4,16]{0,2,1:T(8,128)}), f32[128,4,16]{0,2,1:T(8,128)S(1)}, u32[]{:S(2)}, u32[]{:S(2)}) %all-to-all-start.2) | async-done | bytes 32800 | tf_op jit(solution)/shard_map/all_to_all | solution.py:127
  222.0 3.3 %all-to-all-start = ((f32[128,4,16]{0,2,1:T(8,128)}), f32[128,4,16]{0,2,1:T(8,128)S(1)}, u32[]{:S(2)}, u32[]{:S(2)}) async-start(f32[128,4,16]{0,2,1:T(8,128)} %bitcast.6), calls=%async_computation.1 | async-start | bytes 65536 | tf_op jit(solution)/shard_map/all_to_all | solution.py:124
  225.3 6.4 %fusion.12 = bf16[128,8,8,128]{3,2,1,0:T(8,128)(2,1)} fusion(bf16[128,8,16,128]{3,2,1,0:T(8,128)(2,1)} %param.17, f32[128,8,8,16]{3,2,1,0:T(8,128)} %copy-done, f32[128,8,8]{2,1,0:T(8,128)S(1)} %get-tuple-element.10, pred[128,16]{1,0:T(8,128)(4,1)S(1)} %broadcast_compare_fusion), kind=kOutput, calls=%fused_computation.18 | convolution fusion | flops 35258368 | bytes 6850560 | tf_op jit(solution)/shard_map/rkgp,rkpd->rkgd/dot_general | solution.py:117
  231.7 2.5 reshape.175
  234.2 2.5 copy.20
  236.8 4.2 %all-to-all-start.1 = ((bf16[128,4,2048]{2,0,1:T(8,128)(2,1)}), bf16[128,4,2048]{2,0,1:T(8,128)(2,1)S(1)}, u32[]{:S(2)}, u32[]{:S(2)}) async-start(bf16[128,4,2048]{2,0,1:T(8,128)(2,1)} %copy.20), calls=%async_computation.2 | async-start | bytes 4194304 | tf_op jit(solution)/shard_map/all_to_all | solution.py:131
  241.1 2.6 mul.135
  243.7 4.9 %mul.136 = f32[128,4,2048]{2,0,1:T(8,128)} reshape(f32[128,4,16,128]{3,2,0,1:T(8,128)} %mul.135) | data formatting | bytes 8388608 | tf_op jit(solution)/shard_map/mul | solution.py:137
  248.6 12.6 %all-to-all-done.1 = bf16[128,4,2048]{2,0,1:T(8,128)(2,1)S(1)} async-done(((bf16[128,4,2048]{2,0,1:T(8,128)(2,1)}), bf16[128,4,2048]{2,0,1:T(8,128)(2,1)S(1)}, u32[]{:S(2)}, u32[]{:S(2)}) %all-to-all-start.1) | async-done | bytes 2097184 | tf_op jit(solution)/shard_map/all_to_all | solution.py:131
  261.3 2.9 %multiply_reduce_fusion = f32[128,2048]{1,0:T(8,128)S(1)} fusion(f32[128,4,2048]{2,0,1:T(8,128)} %mul.136, bf16[128,4,2048]{2,0,1:T(8,128)(2,1)S(1)} %all-to-all-done.1), kind=kLoop, calls=%fused_computation.1 | loop fusion | flops 2883584 | bytes 7340032 | tf_op jit(solution)/shard_map/reduce_sum | solution.py:136
  (45 shorter events, 15.3 us)
Async XLA Ops:
  7.2 52.3 %all-gather.6.cloned.1.call-start = ((), (), s32[]{:S(2)}) async-start(), calls=%async_computation.5 | async-start | bytes 4718592 | tf_op jit(solution)/shard_map/all_gather | solution.py:70
  7.9 94.5 %all-gather.4.cloned.1.call-start = ((), (), s32[]{:S(2)}) async-start(), calls=%async_computation.4 | async-start | bytes 2621440 | tf_op jit(solution)/shard_map/all_gather | solution.py:65
  8.6 143.3 %reduce-scatter.2.cloned.1.call-start = ((), (), s32[]{:S(2)}) async-start(), calls=%async_computation.6 | async-start | bytes 4718592 | tf_op jit(solution)/shard_map/reduce_scatter | solution.py:81
  101.4 0.7 copy-start.3
  169.1 39.1 %copy-start.2 = (bf16[128,2048]{1,0:T(8,128)(2,1)}, bf16[128,2048]{1,0:T(8,128)(2,1)S(1)}, u32[]{:S(2)}) copy-start(bf16[128,2048]{1,0:T(8,128)(2,1)S(1)} %get-tuple-element.5) | copy-start | bytes 1572868
  169.1 15.8 %collective-permute-start = (bf16[128,2048]{1,0:T(8,128)(2,1)S(1)}, bf16[128,2048]{1,0:T(8,128)(2,1)S(1)}, u32[]{:S(2)}, u32[]{:S(2)}) collective-permute-start(bf16[128,2048]{1,0:T(8,128)(2,1)S(1)} %get-tuple-element.5), channel_id=1, source_target_pairs={{0,1},{1,2},{2,3},{3,0},{4,5},{5,6},{6,7},{7,4},{8,9},{9,10},{10,1... | collective-permute-start | bytes 1572872 | tf_op jit(solution)/shard_map/ppermute | solution.py:97
  170.6 25.7 %collective-permute-start.1 = (bf16[128,2048]{1,0:T(8,128)(2,1)S(1)}, bf16[128,2048]{1,0:T(8,128)(2,1)}, u32[]{:S(2)}, u32[]{:S(2)}) collective-permute-start(bf16[128,2048]{1,0:T(8,128)(2,1)S(1)} %get-tuple-element.5), channel_id=1, source_target_pairs={{0,3},{1,0},{2,1},{3,2},{4,7},{5,4},{6,5},{7,6},{8,11},{9,8},{10,9... | collective-permute-start | bytes 1572872 | tf_op jit(solution)/shard_map/ppermute | solution.py:100
  184.9 19.2 %collective-permute-start.2 = (bf16[128,2048]{1,0:T(8,128)(2,1)S(1)}, bf16[128,2048]{1,0:T(8,128)(2,1)}, u32[]{:S(2)}, u32[]{:S(2)}) collective-permute-start(bf16[128,2048]{1,0:T(8,128)(2,1)S(1)} %collective-permute-done), channel_id=1, source_target_pairs={{0,1},{1,2},{2,3},{3,0},{4,5},{5,6},{6,7},{7,4},{8,9},{9,10},{10,1... | collective-permute-start | bytes 1572872 | tf_op jit(solution)/shard_map/ppermute | solution.py:97
  185.6 20.2 %copy-start.1 = (bf16[128,8,16,128]{3,2,1,0:T(8,128)(2,1)S(1)}, bf16[128,8,16,128]{3,2,1,0:T(8,128)(2,1)}, u32[]{:S(2)}) copy-start(bf16[128,8,16,128]{3,2,1,0:T(8,128)(2,1)} %param.16) | copy-start | bytes 12582916
  208.2 1.9 copy-start
  214.0 8.0 %all-to-all-start.2 = ((f32[128,4,16]{0,2,1:T(8,128)}), f32[128,4,16]{0,2,1:T(8,128)S(1)}, u32[]{:S(2)}, u32[]{:S(2)}) async-start(f32[128,4,16]{0,2,1:T(8,128)} %bitcast.7), calls=%async_computation.3 | async-start | bytes 65536 | tf_op jit(solution)/shard_map/all_to_all | solution.py:127
  222.0 14.7 %all-to-all-start = ((f32[128,4,16]{0,2,1:T(8,128)}), f32[128,4,16]{0,2,1:T(8,128)S(1)}, u32[]{:S(2)}, u32[]{:S(2)}) async-start(f32[128,4,16]{0,2,1:T(8,128)} %bitcast.6), calls=%async_computation.1 | async-start | bytes 65536 | tf_op jit(solution)/shard_map/all_to_all | solution.py:124
  236.8 24.5 %all-to-all-start.1 = ((bf16[128,4,2048]{2,0,1:T(8,128)(2,1)}), bf16[128,4,2048]{2,0,1:T(8,128)(2,1)S(1)}, u32[]{:S(2)}, u32[]{:S(2)}) async-start(bf16[128,4,2048]{2,0,1:T(8,128)(2,1)} %copy.20), calls=%async_computation.2 | async-start | bytes 4194304 | tf_op jit(solution)/shard_map/all_to_all | solution.py:131
Sparse Core Ops, SparseCore 0:
  9.6 49.8 all-gather.5
  61.3 38.8 all-gather.3
  102.5 49.4 reduce-scatter.1
